TPU v7x, 32 devices: a whole 2x2x4 slice. The times are simulated.
32 devices in a mesh: dp: 4 (over y, x), mp: 8 (over z, core).
Axes of the slice: x: 2, y: 2, z: 4, core: 2. Of those that a mesh axis runs over, the one named last changes fastest.
Arguments:
- tokens: bfloat16 [8192, 2048], P(('dp', 'mp')), may hold values from -6 to 6
- ln1_gain: float32 [2048], replicated, may hold values from 0.5 to 1.5
- ln1_bias: float32 [2048], replicated, may hold values from -1.75 to 1.75
- w_query: bfloat16 [2048, 2048], P(None, 'mp'), may hold values from -0.125 to 0.125
- b_query: float32 [2048], P('mp'), may hold values from -3 to 3
- w_key: bfloat16 [2048, 2048], P(None, 'mp'), may hold values from -0.125 to 0.125
- w_value: bfloat16 [2048, 2048], P(None, 'mp'), may hold values from -0.125 to 0.125
- b_value: float32 [2048], P('mp'), may hold values from -0.125 to 0.125
- w_out: bfloat16 [2048, 2048], P('mp'), may hold values from -2 to 2
- b_out: float32 [2048], replicated, may hold values from -3 to 3
- ln2_gain: float32 [2048], replicated, may hold values from 0.5 to 1.5
- ln2_bias: float32 [2048], replicated, may hold values from -1.75 to 1.75
- w_up: bfloat16 [2048, 8192], P(None, 'mp'), may hold values from -0.125 to 0.125
- b_up: float32 [8192], P('mp'), may hold values from -3 to 3
- w_down: bfloat16 [8192, 2048], P('mp'), may hold values from -0.0625 to 0.0625
- b_down: float32 [2048], replicated, may hold values from -3 to 3
- cotangent: bfloat16 [8192, 2048], P(('dp', 'mp')), may hold values from -6 to 6
- seq_ids: int32 [4, 2048], P('dp'), may hold values from 0 to 2, as said below
- block_mask: int32 [4, 8, 8], P('dp'), may hold values from 0 to 1, as said below
- counts: int32 [4], replicated, may hold values from 512 to 2048, as said below
Outputs:
- output: float32 [8192, 2048], P(('dp', 'mp'))
- grad_in: float32 [8192, 2048], P(('dp', 'mp'))
- grad_ln1_gain: float32 [2048], replicated
- grad_ln1_bias: float32 [2048], replicated
- grad_w_query: float32 [2048, 2048], P(None, 'mp')
- grad_b_query: float32 [2048], P('mp')
- grad_w_key: float32 [2048, 2048], P(None, 'mp')
- grad_w_value: float32 [2048, 2048], P(None, 'mp')
- grad_b_value: float32 [2048], P('mp')
- grad_w_out: float32 [2048, 2048], P('mp')
- grad_b_out: float32 [2048], replicated
- grad_ln2_gain: float32 [2048], replicated
- grad_ln2_bias: float32 [2048], replicated
- grad_w_up: float32 [2048, 8192], P(None, 'mp')
- grad_b_up: float32 [8192], P('mp')
- grad_w_down: float32 [8192, 2048], P('mp')
- grad_b_down: float32 [2048], replicated
Inputs may be any that keep to these rules, and one draw needn't show every extreme that they name: `counts`: one group's count equals 2048 in every draw. `seq_ids`: in group g, slots before a cut carry 0, slots from the cut up to counts[g] - 1 carry 1, later slots carry 2; the cut lies between max(counts[g] - 2048, counts[g] // 2) and min(counts[g], 2048). `block_mask`: diagonal entries are 1 and entries above the diagonal are 0.
All inputs are finite; a program needn't handle non-finite values.
Results may differ from a plain program's by a relative error of at most 0.012.
Values may be sent and summed in bfloat16 or wider, within the bound.
No kernel may reach another device: no remote copies, remote signals or barrier semaphores. Data moves between devices by JAX's collectives and lax.ppermute only.
A program may use at most 256 MiB of HBM per device.

v0:
```python
import jax
import jax.numpy as jnp
from jax import lax
from jax.sharding import PartitionSpec as P

HD = 128
BLOCK = 256
epsilon = 1e-05


def layer_norm(values, gain, bias):
    average = jnp.mean(values, axis=-1, keepdims=True)
    centered = values - average
    variance = jnp.mean(centered * centered, axis=-1, keepdims=True)
    return centered * lax.rsqrt(variance + epsilon) * gain + bias


def inner_rows(left, right):
    return lax.dot_general(
        left, right, (((0,), (0,)), ((), ())), preferred_element_type=jnp.float32
    )


def times_transpose(left, right):
    return lax.dot_general(
        left, right, (((1,), (1,)), ((), ())), preferred_element_type=jnp.float32
    )


def allowed_rows(offset, number, seq_row, mask_table):
    group_tokens = seq_row.shape[0]
    table_width = mask_table.shape[1]
    query_pos = offset + jnp.arange(number, dtype=jnp.int32)
    key_pos = jnp.arange(group_tokens, dtype=jnp.int32)
    query_seq = lax.dynamic_slice_in_dim(seq_row, offset, number)
    table_rows = lax.dynamic_slice_in_dim(mask_table, offset // BLOCK, number // BLOCK, 0)
    spread = jnp.broadcast_to(
        table_rows[:, None, :, None], (number // BLOCK, BLOCK, table_width, BLOCK)
    ).reshape(number, group_tokens)
    return (
        (key_pos[None, :] <= query_pos[:, None])
        & (query_seq[:, None] == seq_row[None, :])
        & (spread == 1)
    )


def on_device(
    tokens,
    ln1_gain,
    ln1_bias,
    w_query,
    b_query,
    w_key,
    w_value,
    b_value,
    w_out,
    b_out,
    ln2_gain,
    ln2_bias,
    w_up,
    b_up,
    w_down,
    b_down,
    cotangent,
    seq_ids,
    block_mask,
    counts,
):
    row_count = tokens.shape[0]
    mp_size = lax.axis_size("mp")
    group_tokens = row_count * mp_size
    local_width = w_query.shape[1]
    local_heads = local_width // HD
    span = min(512, group_tokens)
    block_total = group_tokens // span
    scaling = HD ** (-0.5)
    seq_row = seq_ids[0]
    mask_table = block_mask[0]
    head_shape = (group_tokens, local_heads, HD)
    inputs = tokens.astype(jnp.float32)
    normed_float, pull_one = jax.vjp(layer_norm, inputs, ln1_gain, ln1_bias)
    normed_one = normed_float.astype(jnp.bfloat16)
    gathered_one = lax.all_gather(normed_one, "mp", axis=0, tiled=True)
    queries = (
        (jnp.dot(gathered_one, w_query, preferred_element_type=jnp.float32) + b_query)
        .astype(jnp.bfloat16)
        .reshape(head_shape)
    )
    key_rows = (
        jnp.dot(gathered_one, w_key, preferred_element_type=jnp.float32)
        .astype(jnp.bfloat16)
        .reshape(head_shape)
    )
    values = (
        (jnp.dot(gathered_one, w_value, preferred_element_type=jnp.float32) + b_value)
        .astype(jnp.bfloat16)
        .reshape(head_shape)
    )

    def forward_block(block_index):
        offset = block_index * span
        query_block = lax.dynamic_slice_in_dim(queries, offset, span, 0)
        scores = (
            jnp.einsum("qhd,khd->hqk", query_block, key_rows, preferred_element_type=jnp.float32)
            * scaling
        )
        allowed = allowed_rows(offset, span, seq_row, mask_table)
        scores = jnp.where(allowed[None], scores, -1e30)
        largest = jnp.max(scores, axis=-1, keepdims=True)
        exponent = jnp.exp(scores - largest)
        totals = jnp.sum(exponent, axis=-1, keepdims=True)
        weights = exponent / totals
        mixed = jnp.einsum(
            "hqk,khd->qhd", weights.astype(jnp.bfloat16), values, preferred_element_type=jnp.float32
        )
        return (
            mixed.reshape(span, local_width).astype(jnp.bfloat16),
            (largest + jnp.log(totals))[..., 0],
        )

    attended_blocks, log_totals = lax.map(forward_block, jnp.arange(block_total, dtype=jnp.int32))
    attended = attended_blocks.reshape(group_tokens, local_width)
    branch = lax.psum_scatter(
        jnp.dot(attended, w_out, preferred_element_type=jnp.float32),
        "mp",
        scatter_dimension=0,
        tiled=True,
    )
    middle = inputs + branch + b_out
    normed_mid, pull_two = jax.vjp(layer_norm, middle, ln2_gain, ln2_bias)
    normed_two = normed_mid.astype(jnp.bfloat16)
    gathered_two = lax.all_gather(normed_two, "mp", axis=0, tiled=True)
    hidden = jnp.dot(gathered_two, w_up, preferred_element_type=jnp.float32) + b_up
    activated_float, pull_gelu = jax.vjp(lambda point: jax.nn.gelu(point, approximate=True), hidden)
    activated = activated_float.astype(jnp.bfloat16)
    result = (
        middle
        + lax.psum_scatter(
            jnp.dot(activated, w_down, preferred_element_type=jnp.float32).astype(jnp.bfloat16),
            "mp",
            scatter_dimension=0,
            tiled=True,
        ).astype(jnp.float32)
        + b_down
    )
    group_index = lax.axis_index("dp")
    place = lax.axis_index("mp")
    dp_size = counts.shape[0]
    count_float = counts.astype(jnp.float32)
    is_here = jnp.arange(dp_size, dtype=jnp.int32) == group_index
    count_here = jnp.sum(jnp.where(is_here, counts, 0))
    weighting = dp_size * jnp.sum(jnp.where(is_here, count_float, 0.0)) / jnp.sum(count_float)
    positions = place * row_count + jnp.arange(row_count, dtype=jnp.int32)
    valid_rows = (positions < count_here).astype(jnp.float32)
    out_cot = cotangent.astype(jnp.float32) * valid_rows[:, None] * weighting
    grad_down_bias = jnp.sum(out_cot, axis=0)
    out_cot_low = out_cot.astype(jnp.bfloat16)
    gathered_cot = lax.all_gather(out_cot_low, "mp", axis=0, tiled=True)
    activated_cot = times_transpose(gathered_cot, w_down)
    grad_down = inner_rows(activated, gathered_cot)
    hidden_cot = pull_gelu(activated_cot)[0].astype(jnp.bfloat16)
    grad_up = inner_rows(gathered_two, hidden_cot)
    grad_up_bias = jnp.sum(hidden_cot, axis=0, dtype=jnp.float32)
    normed_two_cot = lax.psum_scatter(
        times_transpose(hidden_cot, w_up), "mp", scatter_dimension=0, tiled=True
    )
    middle_part, grad_gain_two, grad_bias_two = pull_two(normed_two_cot)
    middle_cot = out_cot + middle_part
    grad_out_bias = jnp.sum(middle_cot, axis=0)
    branch_cot = middle_cot.astype(jnp.bfloat16)
    gathered_branch = lax.all_gather(branch_cot, "mp", axis=0, tiled=True)
    attended_cot = times_transpose(gathered_branch, w_out).astype(jnp.bfloat16)
    grad_out = inner_rows(attended, gathered_branch)
    attended_cot = attended_cot.reshape(head_shape)

    def backward_block(carry, block_index):
        key_grad, value_grad = carry
        offset = block_index * span
        query_block = lax.dynamic_slice_in_dim(queries, offset, span, 0)
        cot_block = lax.dynamic_slice_in_dim(attended_cot, offset, span, 0)
        log_here = lax.dynamic_index_in_dim(log_totals, block_index, 0, keepdims=False)
        scores = (
            jnp.einsum("qhd,khd->hqk", query_block, key_rows, preferred_element_type=jnp.float32)
            * scaling
        )
        allowed = allowed_rows(offset, span, seq_row, mask_table)
        weights = jnp.where(allowed[None], jnp.exp(scores - log_here[..., None]), 0.0)
        weight_cot = jnp.einsum(
            "qhd,khd->hqk", cot_block, values, preferred_element_type=jnp.float32
        )
        centre = jnp.sum(weights * weight_cot, axis=-1, keepdims=True)
        score_cot = (weights * (weight_cot - centre)).astype(jnp.bfloat16)
        query_grad = (
            jnp.einsum("hqk,khd->qhd", score_cot, key_rows, preferred_element_type=jnp.float32)
            * scaling
        )
        key_grad = (
            key_grad
            + jnp.einsum("hqk,qhd->khd", score_cot, query_block, preferred_element_type=jnp.float32)
            * scaling
        )
        value_grad = value_grad + jnp.einsum(
            "hqk,qhd->khd",
            weights.astype(jnp.bfloat16),
            cot_block,
            preferred_element_type=jnp.float32,
        )
        return ((key_grad, value_grad), query_grad)

    zeros_start = jnp.zeros(head_shape, jnp.float32)
    (key_grad, value_grad), query_blocks = lax.scan(
        backward_block, (zeros_start, zeros_start), jnp.arange(block_total, dtype=jnp.int32)
    )
    query_low = query_blocks.reshape(group_tokens, local_width).astype(jnp.bfloat16)
    key_low = key_grad.reshape(group_tokens, local_width).astype(jnp.bfloat16)
    value_low = value_grad.reshape(group_tokens, local_width).astype(jnp.bfloat16)
    grad_query = inner_rows(gathered_one, query_low)
    grad_query_bias = jnp.sum(query_low, axis=0, dtype=jnp.float32)
    grad_key = inner_rows(gathered_one, key_low)
    grad_value = inner_rows(gathered_one, value_low)
    grad_value_bias = jnp.sum(value_low, axis=0, dtype=jnp.float32)
    normed_one_cot = lax.psum_scatter(
        times_transpose(query_low, w_query)
        + times_transpose(key_low, w_key)
        + times_transpose(value_low, w_value),
        "mp",
        scatter_dimension=0,
        tiled=True,
    )
    input_part, grad_gain_one, grad_bias_one = pull_one(normed_one_cot)
    grad_input = middle_cot + input_part
    small = lax.psum(
        (grad_gain_one, grad_bias_one, grad_out_bias, grad_gain_two, grad_bias_two, grad_down_bias),
        ("dp", "mp"),
    )
    large = lax.psum(
        (
            grad_query,
            grad_query_bias,
            grad_key,
            grad_value,
            grad_value_bias,
            grad_out,
            grad_up,
            grad_up_bias,
            grad_down,
        ),
        "dp",
    )
    return (
        result,
        grad_input,
        small[0],
        small[1],
        large[0],
        large[1],
        large[2],
        large[3],
        large[4],
        large[5],
        small[2],
        small[3],
        small[4],
        large[6],
        large[7],
        large[8],
        small[5],
    )


def solution(mesh):
    return jax.shard_map(
        on_device,
        mesh=mesh,
        in_specs=(
            P(("dp", "mp"), None),
            P(),
            P(),
            P(None, "mp"),
            P("mp"),
            P(None, "mp"),
            P(None, "mp"),
            P("mp"),
            P("mp", None),
            P(),
            P(),
            P(),
            P(None, "mp"),
            P("mp"),
            P("mp", None),
            P(),
            P(("dp", "mp"), None),
            P("dp", None),
            P("dp", None, None),
            P(),
        ),
        out_specs=(
            P(("dp", "mp"), None),
            P(("dp", "mp"), None),
            P(),
            P(),
            P(None, "mp"),
            P("mp"),
            P(None, "mp"),
            P(None, "mp"),
            P("mp"),
            P("mp", None),
            P(),
            P(),
            P(),
            P(None, "mp"),
            P("mp"),
            P("mp", None),
            P(),
        ),
        check_vma=False,
    )
```

profile of v0, /device:TPU:0, one launch (start us, length us, event | category | flops | bytes accessed | tf_op | source)
XLA Modules:
  0.0 1679.2 jit_solution(10199350876054711192)
XLA Ops:
  14.4 84.8 %all-gather.5.cloned.1.call-done = bf16[2048,2048]{1,0:T(8,128)(2,1)} async-done(((bf16[256,2048]{1,0:T(8,128)(2,1)}), bf16[2048,2048]{1,0:T(8,128)(2,1)}) %all-gather.5.cloned.1.call-update) | async-done | bytes 8388624 | tf_op jit(solution)/shard_map/all_gather | solution.py:83
  99.2 6.7 convolution_convert_fusion.2
  107.6 6.7 fusion.51
  116.0 7.0 fusion.52
  123.0 54.4 %while.31 = (s32[]{:T(128)}, bf16[4,512,256]{2,1,0:T(8,128)(2,1)}, f32[4,2,512]{2,1,0:T(2,128)S(1)}, s32[4]{0:T(128)S(1)}, s32[2048]{0:T(1024)S(1)}, /*index=5*/...) while((s32[]{:T(128)}, bf16[4,512,256]{2,1,0:T(8,128)(2,1)}, ...), condition=%wide.region_5.6_spmd, body=%wide.region_2.5_spmd.sunk | while | flops 1103232512 | bytes 41470496 | solution.py:121
  177.4 9.7 fusion.82
  187.2 166.7 %reduce-scatter.5.cloned.1.call-done = f32[256,2048]{1,0:T(8,128)} async-done(((f32[2048,2048]{1,0:T(8,128)}), f32[256,2048]{1,0:T(8,128)}) %reduce-scatter.5.cloned.1.call-update) | async-done | bytes 2097168 | tf_op jit(solution)/shard_map/reduce_scatter | solution.py:123
  363.3 76.0 %all-gather.7.cloned.1.call-done = bf16[2048,2048]{1,0:T(8,128)(2,1)} async-done(((bf16[256,2048]{1,0:T(8,128)(2,1)}), bf16[2048,2048]{1,0:T(8,128)(2,1)}) %all-gather.7.cloned.1.call-update) | async-done | bytes 8388624 | tf_op jit(solution)/shard_map/all_gather | solution.py:132
  439.3 14.7 fusion.83
  454.0 67.9 %all-gather.9.cloned.1.call-done = bf16[2048,2048]{1,0:T(8,128)(2,1)} async-done(((bf16[256,2048]{1,0:T(8,128)(2,1)}), bf16[2048,2048]{1,0:T(8,128)(2,1)}) %all-gather.9.cloned.1.call-update) | async-done | bytes 8388624 | tf_op jit(solution)/shard_map/all_gather | solution.py:158
  521.9 20.8 %convert_reduce_fusion = (f32[1024]{0:T(1024)}, bf16[2048,1024]{1,0:T(8,128)(2,1)S(1)}) fusion(f32[2048,1024]{1,0:T(8,128)} %fusion.83, f32[1024]{0:T(1024)S(1)} %copy-done.50, bf16[2048,2048]{1,0:T(8,128)(2,1)} %all-gather.9.cloned.1.call-done, bf16[1024,2048]{1,0:T(8,128)(2,1)} %param.38), kind=kOutput, calls=%fused_computation.62 | convolution fusion | flops 8638168064 | bytes 25174016 | tf_op jit(solution)/shard_map/dot_general | solution.py:25
  544.8 12.3 fusion.84
  557.1 15.4 convolution_convert_fusion
  572.6 151.2 %reduce-scatter.9.cloned.1.call-done = f32[256,2048]{1,0:T(8,128)} async-done(((f32[2048,2048]{1,0:T(8,128)}), f32[256,2048]{1,0:T(8,128)}) %reduce-scatter.9.cloned.1.call-update) | async-done | bytes 2097168 | tf_op jit(solution)/shard_map/reduce_scatter | solution.py:164
  727.4 87.2 %reduce-scatter.7.cloned.1.call-done = bf16[256,2048]{1,0:T(8,128)(2,1)} async-done(((bf16[2048,2048]{1,0:T(8,128)(2,1)}), bf16[256,2048]{1,0:T(8,128)(2,1)}) %reduce-scatter.7.cloned.1.call-update) | async-done | bytes 1048592 | tf_op jit(solution)/shard_map/reduce_scatter | solution.py:138
  814.6 4.5 fusion.79
  823.8 78.8 %all-gather.11.cloned.1.call-done = bf16[2048,2048]{1,0:T(8,128)(2,1)} async-done(((bf16[256,2048]{1,0:T(8,128)(2,1)}), bf16[2048,2048]{1,0:T(8,128)(2,1)}) %all-gather.11.cloned.1.call-update) | async-done | bytes 8388624 | tf_op jit(solution)/shard_map/all_gather | solution.py:171
  902.6 6.7 convolution_convert_fusion.1
  909.3 88.9 %while.32 = (s32[]{:T(128)}, f32[2048,2,128]{0,2,1:T(8,128)}, f32[2048,2,128]{0,2,1:T(8,128)}, bf16[4,512,2,128]{3,1,2,0:T(8,128)(2,1)}, s32[4]{0:T(128)S(1)}, /...) while((s32[]{:T(128)}, f32[2048,2,128]{0,2,1:T(8,128)}, ...), condition=%wide.region_18.19_spmd.clone, body=%wide.region_16.18_spmd.clone.sunk | while | flops 2722758144 | bytes 118012680 | solution.py:211
  937.5 4.8 fusion.169
  960.0 4.8 fusion.169
  982.5 4.8 fusion.169
  1004.2 8.2 fusion.85
  1012.4 8.1 fusion.65
  1020.6 18.4 %add_add_fusion = f32[2048,2048]{1,0:T(8,128)} fusion(f32[2048,2048]{1,0:T(8,128)} %fusion.65, f32[2048,2048]{1,0:T(8,128)} %fusion.85, bf16[2048,256]{0,1:T(8,128)(2,1)S(1)} %bitcast.145, bf16[2048,256]{1,0:T(8,128)(2,1)} %param.30), kind=kOutput, calls=%fused_computation.52 | convolution fusion | flops 2155872256 | bytes 52428800 | tf_op jit(solution)/shard_map/dot_general | solution.py:25
  1039.1 15.2 fusion.89
  1054.4 19.1 %fusion.76 = f32[1024,2048]{1,0:T(8,128)} fusion(bf16[2048,2048]{1,0:T(8,128)(2,1)} %all-gather.9.cloned.1.call-done, f32[2048,1024]{1,0:T(8,128)} %fusion.83, f32[1024]{0:T(1024)S(1)} %copy-done.51), kind=kOutput, calls=%fused_computation.125 | convolution fusion | flops 8610906112 | bytes 25169920 | tf_op jit(solution)/shard_map/dot_general | solution.py:19
  1073.6 7.2 fusion.88
  1093.8 10.9 all-reduce.1
  1104.7 101.2 %reduce-scatter.11.cloned.1.call-done = f32[256,2048]{1,0:T(8,128)} async-done(((f32[2048,2048]{1,0:T(8,128)}), f32[256,2048]{1,0:T(8,128)}) %reduce-scatter.11.cloned.1.call-update) | async-done | bytes 2097168 | tf_op jit(solution)/shard_map/reduce_scatter | solution.py:222
  1213.4 40.2 %all-reduce = (f32[2048]{0:T(1024)}, f32[2048]{0:T(1024)}, f32[2048]{0:T(1024)}, f32[2048]{0:T(1024)}, f32[2048]{0:T(1024)}, /*index=5*/f32[2048]{0:T(1024)}) all-reduce(f32[2048]{0:T(1024)S(1)} %get-tuple-element.403, f32[2048]{0:T(1024)S(1)} %get-tuple-element.406, ...), channel_id=1, replica_groups=mesh['dp'=4,'mp'=8] {'dp','mp'}, use_global_device_ids=true, to_apply=%region_23.24 | all-reduce | flops 12288 | bytes 98304 | tf_op jit(solution)/shard_map/psum | solution.py:232
  1253.6 400.9 %all-reduce.5.cloned.1.call-done = (f32[2048,256]{1,0:T(8,128)}, f32[2048,256]{1,0:T(8,128)}, f32[2048,256]{1,0:T(8,128)}, f32[256,2048]{1,0:T(8,128)}, f32[2048,1024]{1,0:T(8,128)}, /*index=5*/f32[1024,2048]{1,0:T(8,128)}) async-done(((f32[2048,256]{1,0:T(8,128)}, f32[2048,256]{1,0:T(8,128)}, f32[2048,256]{1,0:T(8,128)}, f32[256,2048]{1,0:T(8,128)}, f32[2048,1024]{1,0:T(8,128)}, ...) | async-done | bytes 25165840 | tf_op jit(solution)/shard_map/psum | solution.py:236
  (336 shorter events, 187.9 us)
Async XLA Ops:
  7.2 170.2 %copy-start = (bf16[256,2048]{1,0:T(8,128)(2,1)S(1)}, bf16[256,2048]{1,0:T(8,128)(2,1)}, u32[]{:S(2)}) copy-start(bf16[256,2048]{1,0:T(8,128)(2,1)} %param.32) | copy-start | bytes 3145732
  7.2 92.0 %copy-start.24 = (bf16[2048,256]{1,0:T(8,128)(2,1)S(1)}, bf16[2048,256]{1,0:T(8,128)(2,1)}, u32[]{:S(2)}) copy-start(bf16[2048,256]{1,0:T(8,128)(2,1)} %param.29) | copy-start | bytes 3145732
  7.2 92.0 %all-gather.5.cloned.1.call-start = ((), (), s32[]{:S(2)}) async-start(), calls=%async_computation.4 | async-start | bytes 9437184 | tf_op jit(solution)/shard_map/all_gather | solution.py:83
  14.3 339.6 %reduce-scatter.5.cloned.1.call-start = ((), (), s32[]{:S(2)}) async-start(), calls=%async_computation.5 | async-start | bytes 18874368 | tf_op jit(solution)/shard_map/reduce_scatter | solution.py:123
  14.4 93.2 %copy-start.26 = (bf16[2048,256]{1,0:T(8,128)(2,1)S(1)}, bf16[2048,256]{1,0:T(8,128)(2,1)}, u32[]{:S(2)}) copy-start(bf16[2048,256]{1,0:T(8,128)(2,1)} %param.27) | copy-start | bytes 3145732
  14.4 93.2 %copy-start.52 = (f32[256]{0:T(256)S(1)}, f32[256]{0:T(256)}, u32[]{:S(2)}) copy-start(f32[256]{0:T(256)} %param.28) | copy-start | bytes 3076
  187.1 166.8 %copy-start.5 = (bf16[256,2048]{1,0:T(8,128)(2,1)S(1)}, bf16[256,2048]{1,0:T(8,128)(2,1)}, u32[]{:S(2)}) copy-start(bf16[256,2048]{1,0:T(8,128)(2,1)} %param.24) | copy-start | bytes 3145732
  187.1 166.8 %copy-start.44 = (f32[2048]{0:T(1024)S(1)}, f32[2048]{0:T(1024)}, u32[]{:S(2)}) copy-start(f32[2048]{0:T(1024)} %param.33) | copy-start | bytes 24580
  187.1 170.1 %copy-start.30 = (f32[2048]{0:T(1024)S(1)}, f32[2048]{0:T(1024)}, u32[]{:S(2)}) copy-start(f32[2048]{0:T(1024)} %param.34) | copy-start | bytes 24580
  187.1 170.1 %copy-start.45 = (f32[2048]{0:T(1024)S(1)}, f32[2048]{0:T(1024)}, u32[]{:S(2)}) copy-start(f32[2048]{0:T(1024)} %param.35) | copy-start | bytes 24580
  187.1 252.2 %all-gather.7.cloned.1.call-start = ((), (), s32[]{:S(2)}) async-start(), calls=%async_computation.6 | async-start | bytes 9437184 | tf_op jit(solution)/shard_map/all_gather | solution.py:132
  358.6 163.2 %all-gather.9.cloned.1.call-start = ((), (), s32[]{:S(2)}) async-start(), calls=%async_computation.8 | async-start | bytes 9437184 | tf_op jit(solution)/shard_map/all_gather | solution.py:158
  362.0 457.2 %copy-start.38 = (f32[256]{0:T(256)}, f32[256]{0:T(256)S(1)}, u32[]{:S(2)}) copy-start(f32[256]{0:T(256)S(1)} %compare_convert_fusion) | copy-start | bytes 3076
  363.3 158.6 %copy-start.50 = (f32[1024]{0:T(1024)S(1)}, f32[1024]{0:T(1024)}, u32[]{:S(2)}) copy-start(f32[1024]{0:T(1024)} %param.37) | copy-start | bytes 12292
  363.3 360.6 %reduce-scatter.9.cloned.1.call-start = ((), (), s32[]{:S(2)}) async-start(), calls=%async_computation.9 | async-start | bytes 18874368 | tf_op jit(solution)/shard_map/reduce_scatter | solution.py:164
  521.9 22.9 %copy-start.49 = (bf16[2048,1024]{1,0:T(8,128)(2,1)S(1)}, bf16[2048,1024]{1,0:T(8,128)(2,1)}, u32[]{:S(2)}) copy-start(bf16[2048,1024]{1,0:T(8,128)(2,1)} %param.36) | copy-start | bytes 12582916
  557.1 257.5 %reduce-scatter.7.cloned.1.call-start = ((), (), s32[]{:S(2)}) async-start(), calls=%async_computation.7 | async-start | bytes 9437184 | tf_op jit(solution)/shard_map/reduce_scatter | solution.py:138
  572.6 242.0 %copy-start.46 = (f32[2048]{0:T(1024)S(1)}, f32[2048]{0:T(1024)}, u32[]{:S(2)}) copy-start(f32[2048]{0:T(1024)} %param.39) | copy-start | bytes 24580
  572.6 330.0 %all-gather.11.cloned.1.call-start = ((), (), s32[]{:S(2)}) async-start(), calls=%async_computation.10 | async-start | bytes 9437184 | tf_op jit(solution)/shard_map/all_gather | solution.py:171
  819.1 90.2 %copy-start.42 = (f32[256]{0:T(256)}, f32[256]{0:T(256)S(1)}, u32[]{:S(2)}) copy-start(f32[256]{0:T(256)S(1)} %negate_multiply_fusion.1) | copy-start | bytes 3076
  821.9 383.9 %reduce-scatter.11.cloned.1.call-start = ((), (), s32[]{:S(2)}) async-start(), calls=%async_computation.11 | async-start | bytes 18874368 | tf_op jit(solution)/shard_map/reduce_scatter | solution.py:222
  1039.1 615.4 %all-reduce.5.cloned.1.call-start = ((), (), s32[]{:S(2)}) async-start(), calls=%async_computation.12 | async-start | bytes 50331648 | tf_op jit(solution)/shard_map/psum | solution.py:236
  1039.1 41.6 %slice-start.4 = ((s8[8388608]{0:T(1024)(128)(4,1)}), s8[4194304]{0:T(1024)(128)(4,1)S(1)}, s32[]{:S(2)}) async-start(s8[8388608]{0:T(1024)(128)(4,1)} %bitcast.162), calls=%async_computation.17 | async-start | bytes 8388608
  1054.4 26.4 %slice-start.5 = ((s8[8388608]{0:T(1024)(128)(4,1)}), s8[4194304]{0:T(1024)(128)(4,1)S(1)}, s32[]{:S(2)}) async-start(s8[8388608]{0:T(1024)(128)(4,1)} %bitcast.162), calls=%async_computation.18 | async-start | bytes 8388608
  1092.3 113.6 %copy-start.6 = (bf16[256,2048]{1,0:T(8,128)(2,1)S(1)}, bf16[256,2048]{1,0:T(8,128)(2,1)}, u32[]{:S(2)}) copy-start(bf16[256,2048]{1,0:T(8,128)(2,1)} %param.24) | copy-start | bytes 3145732
  1092.3 113.6 %copy-start.29 = (f32[2048]{0:T(1024)S(1)}, f32[2048]{0:T(1024)}, u32[]{:S(2)}) copy-start(f32[2048]{0:T(1024)} %param.25) | copy-start | bytes 24580
  1092.3 113.6 %copy-start.32 = (f32[256]{0:T(256)S(1)}, f32[256]{0:T(256)}, u32[]{:S(2)}) copy-start(f32[256]{0:T(256)} %copy-done.31) | copy-start | bytes 3076
  1093.5 114.6 %copy-start.41 = (f32[256]{0:T(256)S(1)}, f32[256]{0:T(256)}, u32[]{:S(2)}) copy-start(f32[256]{0:T(256)} %copy-done.40) | copy-start | bytes 3076
  1093.5 114.7 %copy-start.37 = (f32[256]{0:T(256)S(1)}, f32[256]{0:T(256)}, u32[]{:S(2)}) copy-start(f32[256]{0:T(256)} %copy-done.36) | copy-start | bytes 3076
  1093.5 115.6 %copy-start.12 = (bf16[256,2048]{1,0:T(8,128)(2,1)S(1)}, bf16[256,2048]{1,0:T(8,128)(2,1)}, u32[]{:S(2)}) copy-start(bf16[256,2048]{1,0:T(8,128)(2,1)} %param.40) | copy-start | bytes 3145732
  1093.5 115.6 %copy-start.39 = (f32[256]{0:T(256)S(1)}, f32[256]{0:T(256)}, u32[]{:S(2)}) copy-start(f32[256]{0:T(256)} %copy-done.38) | copy-start | bytes 3076
  1093.5 115.6 %copy-start.43 = (f32[256]{0:T(256)S(1)}, f32[256]{0:T(256)}, u32[]{:S(2)}) copy-start(f32[256]{0:T(256)} %copy-done.42) | copy-start | bytes 3076
  (59 other events, 226.4 us)
Sparse Core Ops, SparseCore 0:
  14.4 84.7 all-gather.4
  187.2 166.6 reduce-scatter.4
  358.8 80.4 all-gather.6
  441.3 80.5 all-gather.8
  557.2 166.6 reduce-scatter.8
  726.6 87.9 reduce-scatter.6
  822.1 80.4 all-gather.10
  1039.2 166.6 reduce-scatter.10
  1211.6 442.9 all-reduce.4
where the time goes:
time: 1690 us; the launch traced here: 1680 us
  waiting for transfers between devices  1210 us (72%)
  matrix products  259 us (15%)
  other arithmetic  64.5 us (4%)
  local copies, waits for them, and re-layouts  58.9 us (3%)
  blocking collectives  51.1 us (3%)
    psum x1, waiting for transfers between devices, on_device(): lax.psum((grad_query, grad_query_bias, grad_key, grad_value, grad_value_b...  401 us
    reduce_scatter x1, waiting for transfers between devices, on_device(): lax.psum_scatter(jnp.dot(attended, w_out, preferred_element_type=jnp.floa...  167 us
    reduce_scatter x1, waiting for transfers between devices, on_device(): lax.psum_scatter(times_transpose(hidden_cot, w_up), 'mp', scatter_dimensi...  151 us
    reduce_scatter x1, waiting for transfers between devices, on_device(): lax.psum_scatter(times_transpose(query_low, w_query) + times_transpose(ke...  101 us
    reduce_scatter x1, waiting for transfers between devices, on_device(): lax.psum_scatter(jnp.dot(activated, w_down, preferred_element_type=jnp.fl...  87.2 us
    all_gather x1, waiting for transfers between devices, on_device(): gathered_one = lax.all_gather(normed_one, 'mp', axis=0, tiled=True)  84.8 us
    all_gather x1, waiting for transfers between devices, on_device(): gathered_branch = lax.all_gather(branch_cot, 'mp', axis=0, tiled=True)  78.8 us
    all_gather x1, waiting for transfers between devices, on_device(): gathered_two = lax.all_gather(normed_two, 'mp', axis=0, tiled=True)  76 us
  transfers between devices with their start and end apart: 9, of which 9 were waited for; matrix products, arithmetic and copies ran while one was open for 6% of the time, Pallas kernels for 0%

commit v1 on v0

--- a/solution.py
+++ b/solution.py
@@ -6,6 +6,29 @@
 HD = 128
 BLOCK = 256
 epsilon = 1e-05
+
+
+def connect_sheets_here(unit, in_dim):
+    unit = jnp.moveaxis(unit, 0, in_dim)
+    u_next = unit.shape
+    return unit.reshape(
+        *u_next[:in_dim], u_next[in_dim] * u_next[in_dim + 1], *u_next[in_dim + 2 :]
+    )
+
+
+def treat_samples(matrix, row_axis):
+    all_values = lax.axis_size(row_axis)
+    b_next = lax.axis_index(row_axis)
+    t1, q_next = (all_values, b_next)
+    reply, value_now = (matrix[None], 1)
+    while value_now < t1:
+        view_out = lax.ppermute(reply, row_axis, [(s, s ^ value_now) for s in range(t1)])
+        tile_out = q_next & value_now == 0
+        w1 = jnp.where(tile_out, reply, view_out)
+        kept_arr = jnp.where(tile_out, view_out, reply)
+        reply = jnp.concatenate([w1, kept_arr])
+        value_now *= 2
+    return reply
 
 
 def layer_norm(values, gain, bias):
@@ -168,7 +191,8 @@
     middle_cot = out_cot + middle_part
     grad_out_bias = jnp.sum(middle_cot, axis=0)
     branch_cot = middle_cot.astype(jnp.bfloat16)
-    gathered_branch = lax.all_gather(branch_cot, "mp", axis=0, tiled=True)
+    u1 = treat_samples(branch_cot, "mp")
+    gathered_branch = connect_sheets_here(u1, 0)
     attended_cot = times_transpose(gathered_branch, w_out).astype(jnp.bfloat16)
     grad_out = inner_rows(attended, gathered_branch)
     attended_cot = attended_cot.reshape(head_shape)

time: 1690 us -> 1860 us (1.10)
  waiting for transfers between devices: 1210 us -> 1370 us
  other arithmetic: 64.5 us -> 85.6 us
    ppermute x0 -> x3, waiting for transfers between devices: none -> 231 us  [treat_samples(): lax.ppermute(reply, row_axis, [(s, s ^ value_now) for s in range(t1)])]
    all_gather x1 -> x0, waiting for transfers between devices: 78.8 us -> none  [on_device(): gathered_branch = lax.all_gather(branch_cot, 'mp', axis=0, tiled=True)]
  transfers between devices with their start and end apart: 9 -> 11, of which waited for: 9 -> 11; matrix products, arithmetic and copies ran while one was open for 6% -> 5% of each run, Pallas kernels for 0% -> 0%
where the time goes in v1:
time: 1860 us
  waiting for transfers between devices  1370 us (74%)
  matrix products  259 us (14%)
  other arithmetic  85.6 us (5%)
  local copies, waits for them, and re-layouts  60.6 us (3%)
  blocking collectives  51.1 us (3%)
    psum x1, waiting for transfers between devices, on_device(): lax.psum((grad_query, grad_query_bias, grad_key, grad_value, grad_value_b...  401 us
    ppermute x3, waiting for transfers between devices, treat_samples(): lax.ppermute(reply, row_axis, [(s, s ^ value_now) for s in range(t1)])  231 us
    reduce_scatter x1, waiting for transfers between devices, on_device(): lax.psum_scatter(jnp.dot(attended, w_out, preferred_element_type=jnp.floa...  167 us
    reduce_scatter x1, waiting for transfers between devices, on_device(): lax.psum_scatter(times_transpose(hidden_cot, w_up), 'mp', scatter_dimensi...  151 us
    reduce_scatter x1, waiting for transfers between devices, on_device(): lax.psum_scatter(times_transpose(query_low, w_query) + times_transpose(ke...  101 us
    reduce_scatter x1, waiting for transfers between devices, on_device(): lax.psum_scatter(jnp.dot(activated, w_down, preferred_element_type=jnp.fl...  87.2 us
    all_gather x1, waiting for transfers between devices, on_device(): gathered_one = lax.all_gather(normed_one, 'mp', axis=0, tiled=True)  84.8 us
    all_gather x1, waiting for transfers between devices, on_device(): gathered_two = lax.all_gather(normed_two, 'mp', axis=0, tiled=True)  76 us
  transfers between devices with their start and end apart: 11, of which 11 were waited for; matrix products, arithmetic and copies ran while one was open for 5% of the time, Pallas kernels for 0%

profile of v1, /device:TPU:0, one launch (start us, length us, event | category | flops | bytes accessed | tf_op | source)
XLA Modules:
  0.0 1855.7 jit_solution(12782029724336403883)
XLA Ops:
  14.5 84.8 %all-gather.4.cloned.1.call-done = bf16[2048,2048]{1,0:T(8,128)(2,1)} async-done(((bf16[256,2048]{1,0:T(8,128)(2,1)}), bf16[2048,2048]{1,0:T(8,128)(2,1)}) %all-gather.4.cloned.1.call-update) | async-done | bytes 8388624 | tf_op jit(solution)/shard_map/all_gather | solution.py:106
  99.3 6.7 convolution_convert_fusion.2
  107.7 6.7 fusion.51
  116.0 7.0 fusion.52
  123.1 54.4 %while.31 = (s32[]{:T(128)}, bf16[4,512,256]{2,1,0:T(8,128)(2,1)}, f32[4,2,512]{2,1,0:T(2,128)S(1)}, s32[4]{0:T(128)S(1)}, s32[2048]{0:T(1024)S(1)}, /*index=5*/...) while((s32[]{:T(128)}, bf16[4,512,256]{2,1,0:T(8,128)(2,1)}, ...), condition=%wide.region_5.6_spmd, body=%wide.region_2.5_spmd.sunk | while | flops 1103232512 | bytes 41470496 | solution.py:144
  177.5 9.8 fusion.81
  187.4 166.7 %reduce-scatter.5.cloned.1.call-done = f32[256,2048]{1,0:T(8,128)} async-done(((f32[2048,2048]{1,0:T(8,128)}), f32[256,2048]{1,0:T(8,128)}) %reduce-scatter.5.cloned.1.call-update) | async-done | bytes 2097168 | tf_op jit(solution)/shard_map/reduce_scatter | solution.py:146
  363.6 76.0 %all-gather.6.cloned.1.call-done = bf16[2048,2048]{1,0:T(8,128)(2,1)} async-done(((bf16[256,2048]{1,0:T(8,128)(2,1)}), bf16[2048,2048]{1,0:T(8,128)(2,1)}) %all-gather.6.cloned.1.call-update) | async-done | bytes 8388624 | tf_op jit(solution)/shard_map/all_gather | solution.py:155
  439.5 14.7 fusion.82
  454.2 67.9 %all-gather.8.cloned.1.call-done = bf16[2048,2048]{1,0:T(8,128)(2,1)} async-done(((bf16[256,2048]{1,0:T(8,128)(2,1)}), bf16[2048,2048]{1,0:T(8,128)(2,1)}) %all-gather.8.cloned.1.call-update) | async-done | bytes 8388624 | tf_op jit(solution)/shard_map/all_gather | solution.py:181
  522.1 20.8 %convert_reduce_fusion = (f32[1024]{0:T(1024)}, bf16[2048,1024]{1,0:T(8,128)(2,1)S(1)}) fusion(f32[2048,1024]{1,0:T(8,128)} %fusion.82, f32[1024]{0:T(1024)S(1)} %copy-done.53, bf16[2048,2048]{1,0:T(8,128)(2,1)} %all-gather.8.cloned.1.call-done, bf16[1024,2048]{1,0:T(8,128)(2,1)} %param.38), kind=kOutput, calls=%fused_computation.63 | convolution fusion | flops 8638168064 | bytes 25174016 | tf_op jit(solution)/shard_map/dot_general | solution.py:48
  545.0 12.1 fusion.83
  557.2 15.5 convolution_convert_fusion
  572.7 151.2 %reduce-scatter.9.cloned.1.call-done = f32[256,2048]{1,0:T(8,128)} async-done(((f32[2048,2048]{1,0:T(8,128)}), f32[256,2048]{1,0:T(8,128)}) %reduce-scatter.9.cloned.1.call-update) | async-done | bytes 2097168 | tf_op jit(solution)/shard_map/reduce_scatter | solution.py:187
  727.5 87.2 %reduce-scatter.7.cloned.1.call-done = bf16[256,2048]{1,0:T(8,128)(2,1)} async-done(((bf16[2048,2048]{1,0:T(8,128)(2,1)}), bf16[256,2048]{1,0:T(8,128)(2,1)}) %reduce-scatter.7.cloned.1.call-update) | async-done | bytes 1048592 | tf_op jit(solution)/shard_map/reduce_scatter | solution.py:161
  829.2 48.0 %collective-permute-done.1 = bf16[2,256,2048]{2,1,0:T(8,128)(2,1)} collective-permute-done((bf16[2,256,2048]{2,1,0:T(8,128)(2,1)}, bf16[2,256,2048]{2,1,0:T(8,128)(2,1)}, u32[]{:S(2)}, u32[]{:S(2)}) %collective-permute-start.1) | collective-permute-done | bytes 2097184 | tf_op jit(solution)/shard_map/ppermute | solution.py:25
  884.9 180.5 %collective-permute-done.2 = bf16[4,256,2048]{2,1,0:T(8,128)(2,1)} collective-permute-done((bf16[4,256,2048]{2,1,0:T(8,128)(2,1)}, bf16[4,256,2048]{2,1,0:T(8,128)(2,1)}, u32[]{:S(2)}, u32[]{:S(2)}) %collective-permute-start.2) | collective-permute-done | bytes 4194336 | tf_op jit(solution)/shard_map/ppermute | solution.py:25
  1065.4 5.7 broadcast_select_fusion.1
  1071.1 7.6 pad_maximum_fusion
  1078.7 6.7 convolution_convert_fusion.1
  1085.4 88.9 %while.32 = (s32[]{:T(128)}, f32[2048,2,128]{0,2,1:T(8,128)}, f32[2048,2,128]{0,2,1:T(8,128)}, bf16[4,512,2,128]{3,1,2,0:T(8,128)(2,1)}, s32[4]{0:T(128)S(1)}, /...) while((s32[]{:T(128)}, f32[2048,2,128]{0,2,1:T(8,128)}, ...), condition=%wide.region_18.19_spmd.clone, body=%wide.region_16.18_spmd.clone.sunk | while | flops 2722758144 | bytes 118012680 | solution.py:235
  1136.1 4.8 fusion.168
  1180.3 8.2 fusion.84
  1188.5 8.2 fusion.65
  1196.7 18.5 add_add_fusion
  1215.3 15.2 fusion.88
  1230.5 19.1 %fusion.75 = f32[1024,2048]{1,0:T(8,128)} fusion(bf16[2048,2048]{1,0:T(8,128)(2,1)} %all-gather.8.cloned.1.call-done, f32[2048,1024]{1,0:T(8,128)} %fusion.82, f32[1024]{0:T(1024)S(1)} %copy-done.54), kind=kOutput, calls=%fused_computation.134 | convolution fusion | flops 8610906112 | bytes 25169920 | tf_op jit(solution)/shard_map/dot_general | solution.py:42
  1249.7 7.2 fusion.87
  1269.9 10.9 all-reduce.1
  1280.8 101.2 %reduce-scatter.11.cloned.1.call-done = f32[256,2048]{1,0:T(8,128)} async-done(((f32[2048,2048]{1,0:T(8,128)}), f32[256,2048]{1,0:T(8,128)}) %reduce-scatter.11.cloned.1.call-update) | async-done | bytes 2097168 | tf_op jit(solution)/shard_map/reduce_scatter | solution.py:246
  1389.6 40.2 %all-reduce = (f32[2048]{0:T(1024)}, f32[2048]{0:T(1024)}, f32[2048]{0:T(1024)}, f32[2048]{0:T(1024)}, f32[2048]{0:T(1024)}, /*index=5*/f32[2048]{0:T(1024)}) all-reduce(f32[2048]{0:T(1024)S(1)} %get-tuple-element.403, f32[2048]{0:T(1024)S(1)} %get-tuple-element.406, ...), channel_id=1, replica_groups=mesh['dp'=4,'mp'=8] {'dp','mp'}, use_global_device_ids=true, to_apply=%region_23.24 | all-reduce | flops 12288 | bytes 98304 | tf_op jit(solution)/shard_map/psum | solution.py:256
  1429.8 400.9 %all-reduce.5.cloned.1.call-done = (f32[2048,256]{1,0:T(8,128)}, f32[2048,256]{1,0:T(8,128)}, f32[2048,256]{1,0:T(8,128)}, f32[256,2048]{1,0:T(8,128)}, f32[2048,1024]{1,0:T(8,128)}, /*index=5*/f32[1024,2048]{1,0:T(8,128)}) async-done(((f32[2048,256]{1,0:T(8,128)}, f32[2048,256]{1,0:T(8,128)}, f32[2048,256]{1,0:T(8,128)}, f32[256,2048]{1,0:T(8,128)}, f32[2048,1024]{1,0:T(8,128)}, ...) | async-done | bytes 25165840 | tf_op jit(solution)/shard_map/psum | solution.py:260
  (351 shorter events, 215.1 us)
Async XLA Ops:
  7.2 170.3 %copy-start = (bf16[256,2048]{1,0:T(8,128)(2,1)S(1)}, bf16[256,2048]{1,0:T(8,128)(2,1)}, u32[]{:S(2)}) copy-start(bf16[256,2048]{1,0:T(8,128)(2,1)} %param.32) | copy-start | bytes 3145732
  7.2 92.1 %copy-start.27 = (bf16[2048,256]{1,0:T(8,128)(2,1)S(1)}, bf16[2048,256]{1,0:T(8,128)(2,1)}, u32[]{:S(2)}) copy-start(bf16[2048,256]{1,0:T(8,128)(2,1)} %param.29) | copy-start | bytes 3145732
  7.2 92.1 %all-gather.4.cloned.1.call-start = ((), (), s32[]{:S(2)}) async-start(), calls=%async_computation.4 | async-start | bytes 9437184 | tf_op jit(solution)/shard_map/all_gather | solution.py:106
  14.4 339.8 %reduce-scatter.5.cloned.1.call-start = ((), (), s32[]{:S(2)}) async-start(), calls=%async_computation.5 | async-start | bytes 18874368 | tf_op jit(solution)/shard_map/reduce_scatter | solution.py:146
  14.4 93.2 %copy-start.29 = (bf16[2048,256]{1,0:T(8,128)(2,1)S(1)}, bf16[2048,256]{1,0:T(8,128)(2,1)}, u32[]{:S(2)}) copy-start(bf16[2048,256]{1,0:T(8,128)(2,1)} %param.27) | copy-start | bytes 3145732
  14.4 93.2 %copy-start.55 = (f32[256]{0:T(256)S(1)}, f32[256]{0:T(256)}, u32[]{:S(2)}) copy-start(f32[256]{0:T(256)} %param.28) | copy-start | bytes 3076
  187.3 166.8 %copy-start.5 = (bf16[256,2048]{1,0:T(8,128)(2,1)S(1)}, bf16[256,2048]{1,0:T(8,128)(2,1)}, u32[]{:S(2)}) copy-start(bf16[256,2048]{1,0:T(8,128)(2,1)} %param.24) | copy-start | bytes 3145732
  187.3 166.8 %copy-start.47 = (f32[2048]{0:T(1024)S(1)}, f32[2048]{0:T(1024)}, u32[]{:S(2)}) copy-start(f32[2048]{0:T(1024)} %param.33) | copy-start | bytes 24580
  187.3 170.1 %copy-start.33 = (f32[2048]{0:T(1024)S(1)}, f32[2048]{0:T(1024)}, u32[]{:S(2)}) copy-start(f32[2048]{0:T(1024)} %param.34) | copy-start | bytes 24580
  187.3 170.1 %copy-start.48 = (f32[2048]{0:T(1024)S(1)}, f32[2048]{0:T(1024)}, u32[]{:S(2)}) copy-start(f32[2048]{0:T(1024)} %param.35) | copy-start | bytes 24580
  187.4 252.2 %all-gather.6.cloned.1.call-start = ((), (), s32[]{:S(2)}) async-start(), calls=%async_computation.6 | async-start | bytes 9437184 | tf_op jit(solution)/shard_map/all_gather | solution.py:155
  358.9 163.2 %all-gather.8.cloned.1.call-start = ((), (), s32[]{:S(2)}) async-start(), calls=%async_computation.8 | async-start | bytes 9437184 | tf_op jit(solution)/shard_map/all_gather | solution.py:181
  362.2 457.0 %copy-start.41 = (f32[256]{0:T(256)}, f32[256]{0:T(256)S(1)}, u32[]{:S(2)}) copy-start(f32[256]{0:T(256)S(1)} %compare_convert_fusion) | copy-start | bytes 3076
  363.5 158.6 %copy-start.53 = (f32[1024]{0:T(1024)S(1)}, f32[1024]{0:T(1024)}, u32[]{:S(2)}) copy-start(f32[1024]{0:T(1024)} %param.37) | copy-start | bytes 12292
  363.5 360.4 %reduce-scatter.9.cloned.1.call-start = ((), (), s32[]{:S(2)}) async-start(), calls=%async_computation.9 | async-start | bytes 18874368 | tf_op jit(solution)/shard_map/reduce_scatter | solution.py:187
  557.1 257.5 %reduce-scatter.7.cloned.1.call-start = ((), (), s32[]{:S(2)}) async-start(), calls=%async_computation.7 | async-start | bytes 9437184 | tf_op jit(solution)/shard_map/reduce_scatter | solution.py:161
  572.7 242.0 %copy-start.49 = (f32[2048]{0:T(1024)S(1)}, f32[2048]{0:T(1024)}, u32[]{:S(2)}) copy-start(f32[2048]{0:T(1024)} %param.39) | copy-start | bytes 24580
  572.7 809.4 %reduce-scatter.11.cloned.1.call-start = ((), (), s32[]{:S(2)}) async-start(), calls=%async_computation.10 | async-start | bytes 18874368 | tf_op jit(solution)/shard_map/reduce_scatter | solution.py:246
  822.0 3.0 collective-permute-start
  829.2 48.0 %collective-permute-start.1 = (bf16[2,256,2048]{2,1,0:T(8,128)(2,1)}, bf16[2,256,2048]{2,1,0:T(8,128)(2,1)}, u32[]{:S(2)}, u32[]{:S(2)}) collective-permute-start(bf16[2,256,2048]{2,1,0:T(8,128)(2,1)} %pad_maximum_fusion.2), channel_id=1, source_target_pairs={{0,2},{1,3},{2,0},{3,1},{4,6},{5,7},{6,4},{7,5},{8,10},{9,11},{10,... | collective-permute-start | bytes 6291464 | tf_op jit(solution)/shard_map/ppermute | solution.py:25
  882.6 182.9 %collective-permute-start.2 = (bf16[4,256,2048]{2,1,0:T(8,128)(2,1)}, bf16[4,256,2048]{2,1,0:T(8,128)(2,1)}, u32[]{:S(2)}, u32[]{:S(2)}) collective-permute-start(bf16[4,256,2048]{2,1,0:T(8,128)(2,1)} %pad_maximum_fusion.1), channel_id=1, source_target_pairs={{0,4},{1,5},{2,6},{3,7},{4,0},{5,1},{6,2},{7,3},{8,12},{9,13},{10,... | collective-permute-start | bytes 12582920 | tf_op jit(solution)/shard_map/ppermute | solution.py:25
  1215.3 615.4 %all-reduce.5.cloned.1.call-start = ((), (), s32[]{:S(2)}) async-start(), calls=%async_computation.11 | async-start | bytes 50331648 | tf_op jit(solution)/shard_map/psum | solution.py:260
  1215.3 41.6 %slice-start.4 = ((s8[8388608]{0:T(1024)(128)(4,1)}), s8[4194304]{0:T(1024)(128)(4,1)S(1)}, s32[]{:S(2)}) async-start(s8[8388608]{0:T(1024)(128)(4,1)} %bitcast.167), calls=%async_computation.16 | async-start | bytes 8388608
  1230.5 26.3 %slice-start.5 = ((s8[8388608]{0:T(1024)(128)(4,1)}), s8[4194304]{0:T(1024)(128)(4,1)S(1)}, s32[]{:S(2)}) async-start(s8[8388608]{0:T(1024)(128)(4,1)} %bitcast.167), calls=%async_computation.17 | async-start | bytes 8388608
  1268.4 113.6 %copy-start.6 = (bf16[256,2048]{1,0:T(8,128)(2,1)S(1)}, bf16[256,2048]{1,0:T(8,128)(2,1)}, u32[]{:S(2)}) copy-start(bf16[256,2048]{1,0:T(8,128)(2,1)} %param.24) | copy-start | bytes 3145732
  1268.4 113.6 %copy-start.32 = (f32[2048]{0:T(1024)S(1)}, f32[2048]{0:T(1024)}, u32[]{:S(2)}) copy-start(f32[2048]{0:T(1024)} %param.25) | copy-start | bytes 24580
  1268.4 113.6 %copy-start.35 = (f32[256]{0:T(256)S(1)}, f32[256]{0:T(256)}, u32[]{:S(2)}) copy-start(f32[256]{0:T(256)} %copy-done.34) | copy-start | bytes 3076
  1269.6 114.7 %copy-start.44 = (f32[256]{0:T(256)S(1)}, f32[256]{0:T(256)}, u32[]{:S(2)}) copy-start(f32[256]{0:T(256)} %copy-done.43) | copy-start | bytes 3076
  1269.6 114.7 %copy-start.40 = (f32[256]{0:T(256)S(1)}, f32[256]{0:T(256)}, u32[]{:S(2)}) copy-start(f32[256]{0:T(256)} %copy-done.39) | copy-start | bytes 3076
  1269.6 115.7 %copy-start.15 = (bf16[256,2048]{1,0:T(8,128)(2,1)S(1)}, bf16[256,2048]{1,0:T(8,128)(2,1)}, u32[]{:S(2)}) copy-start(bf16[256,2048]{1,0:T(8,128)(2,1)} %param.40) | copy-start | bytes 3145732
  1269.6 115.7 %copy-start.42 = (f32[256]{0:T(256)S(1)}, f32[256]{0:T(256)}, u32[]{:S(2)}) copy-start(f32[256]{0:T(256)} %copy-done.41) | copy-start | bytes 3076
  1269.6 115.7 %copy-start.46 = (f32[256]{0:T(256)S(1)}, f32[256]{0:T(256)}, u32[]{:S(2)}) copy-start(f32[256]{0:T(256)} %copy-done.45) | copy-start | bytes 3076
  (64 other events, 263.8 us)
Sparse Core Ops, SparseCore 0:
  14.5 84.7 all-gather.3
  187.5 166.6 reduce-scatter.4
  359.0 80.4 all-gather.5
  441.6 80.5 all-gather.7
  557.3 166.6 reduce-scatter.8
  726.7 87.9 reduce-scatter.6
  1215.4 166.6 reduce-scatter.10
  1387.7 442.9 all-reduce.4
